TPU v7x, 32 devices: a whole 2x2x4 slice. The times are simulated.
32 devices in a mesh: groups: 2 (over x), lon: 16 (over z, y, core).
Axes of the slice: x: 2, y: 2, z: 4, core: 2. Of those that a mesh axis runs over, the one named last changes fastest.
Arguments:
- scene: bfloat16 [4, 48, 128, 320], P('groups', None, 'lon'), parts along dimension 0, may hold values from -24 to 24
- grad_out: bfloat16 [4, 48, 128, 320], P('groups', None, 'lon'), parts along dimension 0, may hold values from -6 to 6
- conv_first: bfloat16 [3, 3, 320, 320], replicated, may hold values from -0.109375 to 0.109375
- conv_second: bfloat16 [3, 3, 320, 320], replicated, may hold values from -0.109375 to 0.109375
- gain_first: float32 [320], replicated, may hold values from 0.25 to 1.75
- shift_first: float32 [320], replicated, may hold values from -3 to 3
- gain_second: float32 [320], replicated, may hold values from 0.25 to 1.75
- shift_second: float32 [320], replicated, may hold values from -3 to 3
Outputs:
- grad_input: bfloat16 [4, 48, 128, 320], P('groups', None, 'lon'), parts along dimension 0
- grad_first: float32 [1843200], P(('groups', 'lon')), parts along dimension 0
- grad_second: float32 [1843200], P(('groups', 'lon')), parts along dimension 0
There are 2 independent parts, one for each index of `groups`. A program takes and returns all parts, laid end to end along the dimension named above; an argument that names none is the same for every part. Nothing has to cross between parts.
All inputs are finite; a program needn't handle non-finite values.
Results may differ from a plain program's by a relative error of at most 0.0031.
Values may be sent and summed in bfloat16 or wider, within the bound.
A program may use at most 128 MiB of HBM per device.

v0:
```python
import jax
import jax.numpy as jnp
from jax import lax
from jax.sharding import PartitionSpec as P

GROUPS = 32


def with_halo(block, sides, width):
    for axis, dim in sides:
        count = lax.axis_size(axis)
        forward = [(i, i + 1) for i in range(count - 1)]
        forward.append((count - 1, 0))
        backward = [(target, source) for source, target in forward]
        low = lax.ppermute(
            lax.slice_in_dim(block, block.shape[dim] - width, None, axis=dim), axis, forward
        )
        high = lax.ppermute(lax.slice_in_dim(block, 0, width, axis=dim), axis, backward)
        block = jnp.concatenate([low, block, high], axis=dim)
    return block


def row_pad(v):
    return jnp.pad(v, ((0, 0), (1, 1), (0, 0), (0, 0)))


def columns(v):
    return with_halo(v, (("lon", 2),), 1)


def patches_of(padded):
    height = padded.shape[1] - 2
    width = padded.shape[2] - 2
    taps = [padded[:, i : i + height, j : j + width, :] for i in range(3) for j in range(3)]
    joined = jnp.concatenate(taps, axis=-1)
    return joined.reshape(-1, joined.shape[-1])


def convolve(padded, kernel):
    chans = kernel.shape[2]
    shape = (padded.shape[0], padded.shape[1] - 2, padded.shape[2] - 2, kernel.shape[3])
    out = jnp.dot(
        patches_of(padded), kernel.reshape(9 * chans, -1), preferred_element_type=jnp.float32
    )
    return out.reshape(shape)


def flipped(kernel):
    return jnp.transpose(kernel[::-1, ::-1], (0, 1, 3, 2))


def group_sums(v):
    grouped = v.reshape(v.shape[0], v.shape[1], v.shape[2], GROUPS, -1)
    return jnp.sum(grouped, axis=(1, 2, 4))


def spread_out(stat, chans):
    return jnp.repeat(stat, chans // GROUPS, axis=1)[:, None, None, :]


def norm_stats(core, count):
    chans = core.shape[-1]
    total, squares = lax.psum((group_sums(core), group_sums(core * core)), "lon")
    mean = total / count
    spread = squares / count - mean * mean
    inverse = 1.0 / jnp.sqrt(spread + 1e-05)
    return (spread_out(mean, chans), spread_out(inverse, chans))


def norm_backward(dact, vhat, inverse, gain, count):
    chans = dact.shape[-1]
    delta = dact * gain
    first, second = lax.psum((group_sums(delta), group_sums(delta * vhat)), "lon")
    return (
        delta - spread_out(first / count, chans) - vhat * spread_out(second / count, chans)
    ) * inverse


def silu_slope(a):
    sig = jax.nn.sigmoid(a)
    return sig * (1.0 + a * (1.0 - sig))


def per_device(
    scene, grad_out, conv_first, conv_second, gain_first, shift_first, gain_second, shift_second
):
    chans = scene.shape[-1]
    count = scene.shape[1] * scene.shape[2] * lax.axis_size("lon") * (chans // GROUPS)
    core_first = scene.astype(jnp.float32)
    mean_first, inv_first = norm_stats(core_first, count)
    act_first = (core_first - mean_first) * inv_first * gain_first + shift_first
    pad_first = row_pad(columns(jax.nn.silu(act_first).astype(jnp.bfloat16)))
    inner = convolve(pad_first, conv_first)
    mean_second, inv_second = norm_stats(inner, count)
    act_second = (inner - mean_second) * inv_second * gain_second + shift_second
    pad_second = row_pad(columns(jax.nn.silu(act_second).astype(jnp.bfloat16)))
    vhat_first = (core_first - mean_first) * inv_first
    vhat_second = (inner - mean_second) * inv_second
    flat_out = grad_out.reshape(-1, chans)
    local_second = jnp.dot(
        patches_of(pad_second).T, flat_out, preferred_element_type=jnp.float32
    ).reshape(-1)
    grad_second = lax.psum_scatter(local_second, "lon", scatter_dimension=0, tiled=True)
    dsilu_second = convolve(row_pad(columns(grad_out)), flipped(conv_second))
    dact_second = dsilu_second * silu_slope(act_second)
    dinner = norm_backward(dact_second, vhat_second, inv_second, gain_second, count).astype(
        jnp.bfloat16
    )
    local_first = jnp.dot(
        patches_of(pad_first).T, dinner.reshape(-1, chans), preferred_element_type=jnp.float32
    ).reshape(-1)
    grad_first = lax.psum_scatter(local_first, "lon", scatter_dimension=0, tiled=True)
    dsilu_first = convolve(row_pad(columns(dinner)), flipped(conv_first))
    dact_first = dsilu_first * silu_slope(act_first)
    dscene = norm_backward(dact_first, vhat_first, inv_first, gain_first, count)
    grad_input = (grad_out.astype(jnp.float32) + dscene).astype(jnp.bfloat16)
    return (grad_input, grad_first, grad_second)


def solution(mesh):
    placed = (
        P("groups", None, "lon", None),
        P("groups", None, "lon", None),
        P(),
        P(),
        P(),
        P(),
        P(),
        P(),
    )
    return jax.shard_map(
        per_device,
        mesh=mesh,
        in_specs=placed,
        out_specs=(P("groups", None, "lon", None), P(("groups", "lon")), P(("groups", "lon"))),
        check_vma=False,
    )
```

profile of v0, /device:TPU:12, one launch (start us, length us, event | category | flops | bytes accessed | tf_op | source)
XLA Modules:
  0.0 390.2 jit_solution(8895518636697408926)
XLA Ops:
  7.2 1.3 convert_reduce_fusion
  8.6 0.1 reduce_sum.89
  8.7 0.1 reduce_sum.95
  9.0 21.1 %all-reduce.9 = (f32[2,32]{1,0:T(2,128)S(1)}, f32[2,32]{1,0:T(2,128)S(1)}) all-reduce(f32[2,32]{1,0:T(2,128)S(1)} %reduce_sum.96, f32[2,32]{1,0:T(2,128)S(1)} %reduce_sum.90), channel_id=1, replica_groups=mesh['groups'=2,'lon'=16] {'lon'}, use_global_device_ids=true, to_apply=%region_5.6 | all-reduce | flops 128 | bytes 1024 | tf_op jit(solution)/shard_map/psum | solution.py:63
  30.1 0.1 mul.134
  30.3 0.1 sub.66
  30.4 1.1 fusion.34
  31.6 0.9 fusion.54
  32.5 0.5 collective-permute-start.2
  33.0 1.2 collective-permute-start.3
  34.2 0.9 fusion.55
  35.1 2.0 collective-permute-start
  37.1 1.3 collective-permute-start.1
  38.4 1.8 reverse_bitcast_fusion.1
  40.3 2.5 copy.28
  42.8 0.7 copy-done.7
  43.5 1.7 fusion.22
  45.1 3.2 pad_maximum_fusion.4
  48.4 8.2 %concatenate.56 = bf16[2,48,8,2880]{3,2,1,0:T(8,128)(2,1)} concatenate(bf16[2,48,8,320]{3,2,1,0:T(8,128)(2,1)S(1)} %get-tuple-element.68, bf16[2,48,8,320]{3,2,1,0:T(8,128)(2,1)S(1)} %get-tuple-element.69, bf16[2,48,8,320]{3,2,1,0:T(8,128)(2,1)} %get-tuple-element.70, bf16[2,48,8,320]{3,2,1,0:T(8,128)(2,1)S(1)} %get-tuple-element.55, bf16[2,48,8,320]{3,2,1,0:T(8,128)(2,1)S(1)} %fusion.34, ...), dimensions={3} | concatenate | bytes 8847360 | tf_op jit(solution)/shard_map/concatenate | solution.py:35
  56.5 5.0 %fusion.56 = f32[768,320]{1,0:T(8,128)S(1)} fusion(bf16[768,2880]{1,0:T(8,128)(2,1)} %bitcast.26, bf16[2880,320]{1,0:T(8,128)(2,1)} %bitcast.27), kind=kOutput, calls=%fused_computation.88 | convolution fusion | flops 1415577600 | bytes 7249920 | tf_op jit(solution)/shard_map/dot_general | solution.py:42
  61.6 15.2 %reshape_reshape.3 = f32[2,48,8,32,10]{4,3,2,1,0:T(8,128)} reshape(f32[768,320]{1,0:T(8,128)S(1)} %fusion.56) | data formatting | bytes 1966080 | tf_op jit(solution)/shard_map/reshape;reshape | solution.py:53
  76.8 7.0 %fusion.45 = (f32[2,32]{1,0:T(2,128)S(1)}, f32[2,32]{1,0:T(2,128)S(1)}) fusion(f32[2,48,8,32,10]{4,3,2,1,0:T(8,128)} %reshape_reshape.3), kind=kLoop, calls=%fused_computation.77 | loop fusion | flops 737152 | bytes 983552 | tf_op jit(solution)/shard_map/reduce_sum | solution.py:54
  83.7 33.5 %all-reduce.8 = (f32[2,32]{1,0:T(2,128)S(1)}, f32[2,32]{1,0:T(2,128)S(1)}) all-reduce(f32[2,32]{1,0:T(2,128)S(1)} %get-tuple-element.4, f32[2,32]{1,0:T(2,128)S(1)} %get-tuple-element.3), channel_id=1, replica_groups=mesh['groups'=2,'lon'=16] {'lon'}, use_global_device_ids=true, to_apply=%region_9.10 | all-reduce | flops 128 | bytes 1024 | tf_op jit(solution)/shard_map/psum | solution.py:63
  117.3 0.1 mul.142
  117.5 0.1 sub.70
  117.6 1.7 fusion.20
  119.3 3.5 pad_maximum_fusion.6
  122.8 8.1 %concatenate.52 = bf16[2,48,8,2880]{3,2,1,0:T(8,128)(2,1)} concatenate(bf16[2,48,8,320]{3,2,1,0:T(8,128)(2,1)S(1)} %get-tuple-element.74, bf16[2,48,8,320]{3,2,1,0:T(8,128)(2,1)} %get-tuple-element.75, bf16[2,48,8,320]{3,2,1,0:T(8,128)(2,1)} %get-tuple-element.76, bf16[2,48,8,320]{3,2,1,0:T(8,128)(2,1)S(1)} %get-tuple-element.59, bf16[2,48,8,320]{3,2,1,0:T(8,128)(2,1)S(1)} %copy-done, ...), dimensions={3} | concatenate | bytes 8847360 | tf_op jit(solution)/shard_map/concatenate | solution.py:35
  130.9 7.0 %fusion.47 = (f32[2,320]{1,0:T(2,128)S(1)}, f32[2,320]{1,0:T(2,128)S(1)}, bf16[2,48,8,320]{3,2,1,0:T(8,128)(2,1)S(1)}, f32[2,48,8,320]{3,2,1,0:T(8,128)}) fusion(f32[2,320]{1,0:T(2,128)S(1)} %mul.142, f32[2,48,8,320]{3,2,1,0:T(8,128)S(1)} %bitcast.24, f32[2,320]{1,0:T(2,128)S(1)} %sub.70, f32[320]{0:T(512)} %param.15, f32[320]{0:T(512)} %param.14, ...), kind=kOutput, calls=%fused_computation.79 | convolution fusion | flops 1420000000 | bytes 8737280 | tf_op jit(solution)/shard_map/dot_general | solution.py:42
  137.9 0.2 fusion.52
  138.2 4.5 %collective-permute-start.7 = (bf16[2,48,1,320]{3,2,1,0:T(2,128)(2,1)S(1)}, bf16[2,48,1,320]{3,2,1,0:T(2,128)(2,1)S(1)}, u32[]{:S(2)}, u32[]{:S(2)}) collective-permute-start(bf16[2,48,1,320]{3,2,1,0:T(2,128)(2,1)S(1)} %get-tuple-element.49), channel_id=1, source_target_pairs={{1,0},{2,1},{3,2},{4,3},{5,4},{6,5},{7,6},{8,7},{9,8},{10,9},{11,1... | collective-permute-start | bytes 184328 | tf_op jit(solution)/shard_map/ppermute | solution.py:18
  142.8 0.1 reduce_sum.126
  143.0 29.6 %all-reduce.7 = (f32[2,32]{1,0:T(2,128)S(1)}, f32[2,32]{1,0:T(2,128)S(1)}) all-reduce(f32[2,32]{1,0:T(2,128)S(1)} %reduce_sum.127, f32[2,32]{1,0:T(2,128)S(1)} %reduce_sum.124), channel_id=1, replica_groups=mesh['groups'=2,'lon'=16] {'lon'}, use_global_device_ids=true, to_apply=%region_15.16 | all-reduce | flops 128 | bytes 1024 | tf_op jit(solution)/shard_map/psum | solution.py:73
  172.8 0.7 mul.152
  173.5 0.7 sub.75
  174.2 1.6 multiply_convert_fusion.1
  175.8 6.9 %fusion.4 = f32[2880,320]{1,0:T(8,128)} fusion(bf16[2,48,8,2880]{3,2,1,0:T(8,128)(2,1)} %concatenate.56, bf16[2,48,8,320]{3,2,1,0:T(8,128)(2,1)S(1)} %multiply_convert_fusion.1), kind=kOutput, calls=%fused_computation.5 | convolution fusion | flops 1415577600 | bytes 8601600 | tf_op jit(solution)/shard_map/dot_general | solution.py:109
  182.7 5.7 %reshape.70 = f32[921600]{0:T(1024)} reshape(f32[2880,320]{1,0:T(8,128)} %fusion.4) | data formatting | bytes 7372800 | tf_op jit(solution)/shard_map/reshape | solution.py:111
  188.4 0.7 copy-done.3
  189.0 0.7 copy-done.5
  189.7 0.8 select_maximum_fusion
  190.5 1.5 fusion.48
  192.0 1.6 pad_maximum_fusion
  193.6 7.8 %concatenate.64 = bf16[2,48,8,2880]{3,2,1,0:T(8,128)(2,1)} concatenate(bf16[2,48,8,320]{3,2,1,0:T(8,128)(2,1)} %get-tuple-element.26, bf16[2,48,8,320]{3,2,1,0:T(8,128)(2,1)} %get-tuple-element.25, bf16[2,48,8,320]{3,2,1,0:T(8,128)(2,1)} %get-tuple-element.24, bf16[2,48,8,320]{3,2,1,0:T(8,128)(2,1)} %get-tuple-element.47, bf16[2,48,8,320]{3,2,1,0:T(8,128)(2,1)S(1)} %get-tuple-element.45, ...), dimensions={3} | concatenate | bytes 8847360 | tf_op jit(solution)/shard_map/concatenate | solution.py:35
  201.4 6.8 %fusion.7 = f32[2880,320]{1,0:T(8,128)} fusion(bf16[2,48,8,2880]{3,2,1,0:T(8,128)(2,1)} %concatenate.64, bf16[2,48,8,320]{3,2,1,0:T(8,128)(2,1)S(1)} %copy-done), kind=kOutput, calls=%fused_computation.6 | convolution fusion | flops 1415577600 | bytes 8601600 | tf_op jit(solution)/shard_map/dot_general | solution.py:100
  208.2 5.7 %reshape.71 = f32[921600]{0:T(1024)} reshape(f32[2880,320]{1,0:T(8,128)} %fusion.7) | data formatting | bytes 7372800 | tf_op jit(solution)/shard_map/reshape | solution.py:102
  213.9 0.9 fusion.53
  214.8 4.4 %collective-permute-start.5 = (bf16[2,48,1,320]{3,2,1,0:T(2,128)(2,1)}, bf16[2,48,1,320]{3,2,1,0:T(2,128)(2,1)}, u32[]{:S(2)}, u32[]{:S(2)}) collective-permute-start(bf16[2,48,1,320]{3,2,1,0:T(2,128)(2,1)} %get-tuple-element.53), channel_id=1, source_target_pairs={{1,0},{2,1},{3,2},{4,3},{5,4},{6,5},{7,6},{8,7},{9,8},{10,9},{11,1... | collective-permute-start | bytes 184328 | tf_op jit(solution)/shard_map/ppermute | solution.py:18
  219.2 1.8 reverse_bitcast_fusion
  221.1 2.5 copy.32
  223.6 0.6 dynamic-slice
  224.9 2.6 pad_maximum_fusion.2
  227.5 1.7 select_maximum_fusion.2
  229.1 1.5 fusion.49
  230.7 7.8 %concatenate.60 = bf16[2,48,8,2880]{3,2,1,0:T(8,128)(2,1)} concatenate(bf16[2,48,8,320]{3,2,1,0:T(8,128)(2,1)} %get-tuple-element.32, bf16[2,48,8,320]{3,2,1,0:T(8,128)(2,1)} %get-tuple-element.31, bf16[2,48,8,320]{3,2,1,0:T(8,128)(2,1)} %get-tuple-element.30, bf16[2,48,8,320]{3,2,1,0:T(8,128)(2,1)} %get-tuple-element.51, bf16[2,48,8,320]{3,2,1,0:T(8,128)(2,1)S(1)} %multiply_convert_fusion.1, ...), dimensions={3} | concatenate | bytes 8847360 | tf_op jit(solution)/shard_map/concatenate | solution.py:35
  238.5 5.5 %fusion.46 = (f32[2,320]{1,0:T(2,128)S(1)}, f32[2,320]{1,0:T(2,128)S(1)}, f32[2,48,8,320]{3,2,1,0:T(8,128)S(1)}) fusion(f32[2,320]{1,0:T(2,128)S(1)} %mul.134, f32[2,320]{1,0:T(2,128)S(1)} %sub.66, bf16[2,48,8,320]{3,2,1,0:T(8,128)(2,1)S(1)} %copy-done.2, f32[320]{0:T(512)S(1)} %copy-done.8, f32[320]{0:T(512)S(1)} %copy-done.9, ...), kind=kOutput, calls=%fused_computation.78 | convolution fusion | flops 1419754240 | bytes 7754240 | tf_op jit(solution)/shard_map/dot_general | solution.py:42
  244.2 0.1 reduce_sum.132
  244.5 35.2 %all-reduce.6 = (f32[2,32]{1,0:T(2,128)S(1)}, f32[2,32]{1,0:T(2,128)S(1)}) all-reduce(f32[2,32]{1,0:T(2,128)S(1)} %reduce_sum.133, f32[2,32]{1,0:T(2,128)S(1)} %reduce_sum.130), channel_id=1, replica_groups=mesh['groups'=2,'lon'=16] {'lon'}, use_global_device_ids=true, to_apply=%region_21.22 | all-reduce | flops 128 | bytes 1024 | tf_op jit(solution)/shard_map/psum | solution.py:73
  279.8 0.1 mul.161
  280.0 0.1 sub.80
  280.1 1.2 fusion.41
  281.3 98.6 %all-reduce.13.cloned.1.call-done = (f32[921600]{0:T(1024)}, f32[921600]{0:T(1024)}) async-done(((f32[921600]{0:T(1024)}, f32[921600]{0:T(1024)}), (f32[921600]{0:T(1024)}, f32[921600]{0:T(1024)})) %all-reduce.13.cloned.1.call-update) | async-done | bytes 7372816
  379.9 1.8 dynamic-slice.1
  381.6 1.8 dynamic-slice.3
  (53 shorter events, 1.5 us)
Async XLA Ops:
  7.2 23.3 %copy-start.1 = (bf16[2,48,8,320]{3,2,1,0:T(8,128)(2,1)S(1)}, bf16[2,48,8,320]{3,2,1,0:T(8,128)(2,1)}, u32[]{:S(2)}) copy-start(bf16[2,48,8,320]{3,2,1,0:T(8,128)(2,1)} %param.8) | copy-start | bytes 1474564
  7.2 27.0 %copy-start = (bf16[2,48,8,320]{3,2,1,0:T(8,128)(2,1)S(1)}, bf16[2,48,8,320]{3,2,1,0:T(8,128)(2,1)}, u32[]{:S(2)}) copy-start(bf16[2,48,8,320]{3,2,1,0:T(8,128)(2,1)} %param.9) | copy-start | bytes 1474564
  7.2 372.7 %all-reduce.13.cloned.1.call-start = ((), (), s32[]{:S(2)}) async-start(), calls=%async_computation | async-start | bytes 14745600
  32.5 10.3 %collective-permute-start.2 = (bf16[2,48,1,320]{3,2,1,0:T(2,128)(2,1)}, bf16[2,48,1,320]{3,2,1,0:T(2,128)(2,1)S(1)}, u32[]{:S(2)}, u32[]{:S(2)}) collective-permute-start(bf16[2,48,1,320]{3,2,1,0:T(2,128)(2,1)} %get-tuple-element.56), channel_id=1, source_target_pairs={{0,1},{1,2},{2,3},{3,4},{4,5},{5,6},{6,7},{7,8},{8,9},{9,10},{10,1... | collective-permute-start | bytes 184328 | tf_op jit(solution)/shard_map/ppermute | solution.py:15
  33.0 9.8 %collective-permute-start.3 = (bf16[2,48,1,320]{3,2,1,0:T(2,128)(2,1)}, bf16[2,48,1,320]{3,2,1,0:T(2,128)(2,1)}, u32[]{:S(2)}, u32[]{:S(2)}) collective-permute-start(bf16[2,48,1,320]{3,2,1,0:T(2,128)(2,1)} %get-tuple-element.57), channel_id=1, source_target_pairs={{1,0},{2,1},{3,2},{4,3},{5,4},{6,5},{7,6},{8,7},{9,8},{10,9},{11,1... | collective-permute-start | bytes 184328 | tf_op jit(solution)/shard_map/ppermute | solution.py:18
  35.1 82.5 %collective-permute-start = (bf16[2,48,1,320]{3,2,1,0:T(2,128)(2,1)}, bf16[2,48,1,320]{3,2,1,0:T(2,128)(2,1)}, u32[]{:S(2)}, u32[]{:S(2)}) collective-permute-start(bf16[2,48,1,320]{3,2,1,0:T(2,128)(2,1)} %get-tuple-element.60), channel_id=1, source_target_pairs={{0,1},{1,2},{2,3},{3,4},{4,5},{5,6},{6,7},{7,8},{8,9},{9,10},{10,1... | collective-permute-start | bytes 184328 | tf_op jit(solution)/shard_map/ppermute | solution.py:15
  37.1 80.5 %collective-permute-start.1 = (bf16[2,48,1,320]{3,2,1,0:T(2,128)(2,1)}, bf16[2,48,1,320]{3,2,1,0:T(2,128)(2,1)}, u32[]{:S(2)}, u32[]{:S(2)}) collective-permute-start(bf16[2,48,1,320]{3,2,1,0:T(2,128)(2,1)} %get-tuple-element.61), channel_id=1, source_target_pairs={{1,0},{2,1},{3,2},{4,3},{5,4},{6,5},{7,6},{8,7},{9,8},{10,9},{11,1... | collective-permute-start | bytes 184328 | tf_op jit(solution)/shard_map/ppermute | solution.py:18
  42.8 0.7 copy-start.7
  138.1 50.3 %collective-permute-start.6 = (bf16[2,48,1,320]{3,2,1,0:T(2,128)(2,1)S(1)}, bf16[2,48,1,320]{3,2,1,0:T(2,128)(2,1)S(1)}, u32[]{:S(2)}, u32[]{:S(2)}) collective-permute-start(bf16[2,48,1,320]{3,2,1,0:T(2,128)(2,1)S(1)} %get-tuple-element.48), channel_id=1, source_target_pairs={{0,1},{1,2},{2,3},{3,4},{4,5},{5,6},{6,7},{7,8},{8,9},{9,10},{10,1... | collective-permute-start | bytes 184328 | tf_op jit(solution)/shard_map/ppermute | solution.py:15
  138.2 50.2 %collective-permute-start.7 = (bf16[2,48,1,320]{3,2,1,0:T(2,128)(2,1)S(1)}, bf16[2,48,1,320]{3,2,1,0:T(2,128)(2,1)S(1)}, u32[]{:S(2)}, u32[]{:S(2)}) collective-permute-start(bf16[2,48,1,320]{3,2,1,0:T(2,128)(2,1)S(1)} %get-tuple-element.49), channel_id=1, source_target_pairs={{1,0},{2,1},{3,2},{4,3},{5,4},{6,5},{7,6},{8,7},{9,8},{10,9},{11,1... | collective-permute-start | bytes 184328 | tf_op jit(solution)/shard_map/ppermute | solution.py:18
  188.4 0.7 copy-start.3
  189.0 0.7 copy-start.5
  190.5 1.5 copy-start.4
  190.5 1.5 copy-start.6
  214.8 10.1 %collective-permute-start.4 = (bf16[2,48,1,320]{3,2,1,0:T(2,128)(2,1)}, bf16[2,48,1,320]{3,2,1,0:T(2,128)(2,1)S(1)}, u32[]{:S(2)}, u32[]{:S(2)}) collective-permute-start(bf16[2,48,1,320]{3,2,1,0:T(2,128)(2,1)} %get-tuple-element.52), channel_id=1, source_target_pairs={{0,1},{1,2},{2,3},{3,4},{4,5},{5,6},{6,7},{7,8},{8,9},{9,10},{10,1... | collective-permute-start | bytes 184328 | tf_op jit(solution)/shard_map/ppermute | solution.py:15
  214.8 10.1 %collective-permute-start.5 = (bf16[2,48,1,320]{3,2,1,0:T(2,128)(2,1)}, bf16[2,48,1,320]{3,2,1,0:T(2,128)(2,1)}, u32[]{:S(2)}, u32[]{:S(2)}) collective-permute-start(bf16[2,48,1,320]{3,2,1,0:T(2,128)(2,1)} %get-tuple-element.53), channel_id=1, source_target_pairs={{1,0},{2,1},{3,2},{4,3},{5,4},{6,5},{7,6},{8,7},{9,8},{10,9},{11,1... | collective-permute-start | bytes 184328 | tf_op jit(solution)/shard_map/ppermute | solution.py:18
  221.1 2.5 copy-start.10
  230.7 7.8 %copy-start.2 = (bf16[2,48,8,320]{3,2,1,0:T(8,128)(2,1)S(1)}, bf16[2,48,8,320]{3,2,1,0:T(8,128)(2,1)}, u32[]{:S(2)}) copy-start(bf16[2,48,8,320]{3,2,1,0:T(8,128)(2,1)} %param.8) | copy-start | bytes 1474564
  230.7 7.8 %copy-start.8 = (f32[320]{0:T(512)S(1)}, f32[320]{0:T(512)}, u32[]{:S(2)}) copy-start(f32[320]{0:T(512)} %param.13) | copy-start | bytes 3844
  230.7 7.9 %copy-start.9 = (f32[320]{0:T(512)S(1)}, f32[320]{0:T(512)}, u32[]{:S(2)}) copy-start(f32[320]{0:T(512)} %param.12) | copy-start | bytes 3844
Sparse Core Ops, SparseCore 0:
  214.0 165.7 all-reduce.12
where the time goes:
time: 395 us; the launch traced here: 390 us
  blocking collectives  119 us (30%)
  waiting for transfers between devices  98.6 us (25%)
  local copies, waits for them, and re-layouts  82.5 us (21%)
  matrix products  31.3 us (8%)
  other arithmetic  29.5 us (7%)
  between operations  15 us (4%)
  starting transfers between devices  14 us (4%)
    unnamed x2, waiting for transfers between devices  98.6 us
    psum x2, blocking collectives, norm_backward(): lax.psum((group_sums(delta), group_sums(delta * vhat)), 'lon')  64.9 us
    psum x2, blocking collectives, norm_stats(): lax.psum((group_sums(core), group_sums(core * core)), 'lon')  54.5 us
    concatenate x4, local copies, waits for them, and re-layouts, patches_of(): joined = jnp.concatenate(taps, axis=-1)  31.9 us
    dot_general x3, matrix products, convolve(): jnp.dot(patches_of(padded), kernel.reshape(9 * chans, -1), preferred_elem...  17.5 us
    concatenate x8, other arithmetic, with_halo(): block = jnp.concatenate([low, block, high], axis=dim)  16.7 us
    another operation x1, local copies, waits for them, and re-layouts, group_sums(): grouped = v.reshape(v.shape[0], v.shape[1], v.shape[2], GROUPS, -1)  15.2 us
    ppermute x4, starting transfers between devices, with_halo(): lax.ppermute(lax.slice_in_dim(block, 0, width, axis=dim), axis, backward)  11.4 us
  transfers between devices with their start and end apart: 9, of which 1 were waited for; matrix products, arithmetic and copies ran while one was open for 23% of the time, Pallas kernels for 0%

commit v1 on v0

v1 whole, which is shorter than its diff:
```python
import functools

import jax
import jax.numpy as jnp
from jax import lax
from jax.experimental import pallas as pl
from jax.experimental.pallas import tpu as pltpu
from jax.sharding import PartitionSpec as P

GROUPS = 32
F32 = jnp.float32
BF16 = jnp.bfloat16
MESH = pl.DeviceIdType.MESH
HIGH = lax.Precision.HIGHEST


def window(rows, n):
    if n % 2 or rows % n or (2 * rows // n) % 8:
        return None
    own = rows // n
    off = own // 8 * 8
    return own, off, 2 * own - off


def sigmoid(a):
    return 1.0 / (1.0 + jnp.exp(-a))


def slope(a):
    sig = sigmoid(a)
    return sig * (1.0 + a * (1.0 - sig))


def kernel(n, height, eps_count, win, *refs):
    (x_ref, g_ref, w1_ref, w2_ref, par_ref, mix_ref, out_ref, d1_ref, d2_ref) = refs[:9]
    (
        st_send, st_recv, ha_send, ha_recv, hb_send, hb_recv, hc_send, hc_recv,
        pad, vbuf, ubuf, gbuf, dbuf, inner, dsil, delta, dinn, coef, vh_halo,
        st_ss, st_rs, h_ss, h_rs,
    ) = refs[9:32]
    pixels, chans = x_ref.shape
    tile = 16 * (height // 3)
    tiles = pixels // tile
    edge_rows = pixels // 8
    me = lax.axis_index("lon")
    right, left = lax.rem(me + 1, n), lax.rem(me + n - 1, n)

    def at(t):
        return pl.ds(pl.multiple_of(t * tile, 16), tile)

    def greet(k, _):
        pl.semaphore_signal(
            barrier, inc=1, device_id={"lon": lax.rem(me + k, n)}, device_id_type=MESH
        )
        return 0

    barrier = pltpu.get_barrier_semaphore()
    lax.fori_loop(1, n, greet, 0)

    def stat_copy(rnd, k):
        return pltpu.make_async_remote_copy(
            src_ref=st_send.at[rnd],
            dst_ref=st_recv.at[rnd, k],
            send_sem=st_ss.at[rnd, k],
            recv_sem=st_rs.at[rnd, k],
            device_id={"lon": lax.rem(me + k, n)},
            device_id_type=MESH,
        )

    def stat_put(rnd, total, second):
        rows = [
            jnp.sum(v[8 * b : 8 * b + 8], axis=0, keepdims=True)
            for v in (total, second)
            for b in range(2)
        ]
        block = jnp.concatenate(rows + [jnp.zeros((4, chans), F32)], axis=0)
        st_send[rnd] = block
        st_recv[rnd, 0] = block

    def stat_start(rnd):
        def go(k, _):
            stat_copy(rnd, k).start()
            return 0

        lax.fori_loop(1, n, go, 0)

    def stat_end(rnd):
        def end(k, _):
            stat_copy(rnd, k).wait()
            return 0

        lax.fori_loop(1, n, end, 0)

        def add(k, acc):
            return acc + st_recv[rnd, k]

        total = lax.fori_loop(1, n, add, st_recv[rnd, 0])
        means = (
            jnp.dot(total, mix_ref[...], precision=HIGH, preferred_element_type=F32)
            * (1.0 / eps_count)
        )
        return [means[r : r + 1] for r in range(4)]

    def halo_copies(rnd, send, recv):
        return [
            pltpu.make_async_remote_copy(
                src_ref=send.at[side],
                dst_ref=recv.at[1 - side],
                send_sem=h_ss.at[rnd, side],
                recv_sem=h_rs.at[rnd, 1 - side],
                device_id={"lon": peer},
                device_id_type=MESH,
            )
            for side, peer in ((0, left), (1, right))
        ]

    def halo_end(rnd, send, recv):
        copies = halo_copies(rnd, send, recv)
        for copy in copies:
            copy.wait_send()
        for copy in copies:
            copy.wait_recv()

    def pick(column, dtype):
        r = lax.broadcasted_iota(jnp.int32, (edge_rows, pixels), 0)
        p = lax.broadcasted_iota(jnp.int32, (edge_rows, pixels), 1)
        return jnp.where(p == 8 * r + column, 1.0, 0.0).astype(dtype)

    def edge(value, column):
        if value.dtype == BF16:
            return jnp.dot(pick(column, BF16), value, preferred_element_type=F32).astype(BF16)
        return jnp.dot(pick(column, F32), value, precision=HIGH, preferred_element_type=F32)

    def both(first, second):
        return jnp.concatenate(
            [jnp.broadcast_to(first, (8, chans)), jnp.broadcast_to(second, (8, chans))], axis=0
        )

    def halo_both(first, second):
        odd = lax.broadcasted_iota(jnp.int32, (edge_rows, chans), 0) & 1
        return jnp.where(odd == 0, first, second)

    def split(v):
        return v.reshape(v.shape[0] // 16, 16, chans)

    def fold(v):
        return jnp.sum(split(v), axis=0)

    def shifts(buf, low, high):
        zero = jnp.zeros((16, chans), BF16)
        for j in range(3):
            buf[j, 0:16] = zero
            buf[j, pixels + 16 : pixels + 32] = zero
        column = lax.broadcasted_iota(jnp.int32, (tile, chans), 0) & 7
        for t in range(tiles):
            p = lax.broadcasted_iota(jnp.int32, (tile, edge_rows), 0) + t * tile
            r = lax.broadcasted_iota(jnp.int32, (tile, edge_rows), 1)
            place = jnp.where((p >> 3) == r, 1.0, 0.0).astype(BF16)
            start = t * tile
            rows = slice(16 + start, 16 + start + tile)
            from_low = jnp.dot(place, low, preferred_element_type=F32)
            from_high = jnp.dot(place, high, preferred_element_type=F32)
            buf[0, rows] = jnp.where(
                column == 0, from_low, pad[start + 7 : start + 7 + tile]
            ).astype(BF16)
            buf[1, rows] = pad[start + 8 : start + 8 + tile].astype(BF16)
            buf[2, rows] = jnp.where(
                column == 7, from_high, pad[start + 9 : start + 9 + tile]
            ).astype(BF16)

    def pad_at(t):
        return pl.ds(pl.multiple_of(t * tile + 8, 8), tile)

    def taps(buf, w_ref, t, transposed):
        acc = jnp.zeros((tile, chans), F32)
        for i in range(3):
            for j in range(3):
                rows = pl.ds(pl.multiple_of(t * tile + 16 * i, 16), tile)
                lhs = buf[j, rows, :]
                if transposed:
                    acc += lax.dot_general(
                        lhs, w_ref[8 - 3 * i - j], (((1,), (1,)), ((), ())),
                        preferred_element_type=F32,
                    )
                else:
                    acc += jnp.dot(lhs, w_ref[3 * i + j], preferred_element_type=F32)
        return acc

    def loop(body):
        def step(t, carry):
            body(t)
            return carry

        lax.fori_loop(0, tiles, step, 0)

    def loop_sums(body):
        zero = jnp.zeros((16, chans), F32)

        def step(t, carry):
            a, b = body(t)
            return carry[0] + a, carry[1] + b

        return lax.fori_loop(0, tiles, step, (zero, zero))

    gain1, shift1 = par_ref[0:1], par_ref[1:2]
    gain2, shift2 = par_ref[2:3], par_ref[3:4]

    def sums_x(t):
        v = x_ref[at(t), :].astype(F32)
        return fold(v), fold(v * v)

    stat_put(0, *loop_sums(sums_x))
    for side, column in ((0, 0), (1, 7)):
        ha_send[side, 0:edge_rows] = edge(x_ref[...], column)
        ha_send[side, edge_rows : 2 * edge_rows] = edge(g_ref[...], column)
    pad[0:8] = jnp.zeros((8, chans), F32)
    pad[pixels + 8 : pixels + 16] = jnp.zeros((8, chans), F32)
    pl.semaphore_wait(barrier, n - 1)
    stat_start(0)
    for copy in halo_copies(0, ha_send, ha_recv):
        copy.start()

    def pad_g(t):
        pad[pad_at(t), :] = g_ref[at(t), :].astype(F32)

    loop(pad_g)
    halo_end(0, ha_send, ha_recv)
    shifts(gbuf, ha_recv[0, edge_rows : 2 * edge_rows], ha_recv[1, edge_rows : 2 * edge_rows])

    def conv_g(t):
        dsil[at(t), :] = taps(gbuf, w2_ref, t, True)

    loop(conv_g)

    def norm_coefs(rnd):
        m0, m1, q0, q1 = stat_end(rnd)
        i0 = 1.0 / jnp.sqrt(q0 - m0 * m0 + 1e-05)
        i1 = 1.0 / jnp.sqrt(q1 - m1 * m1 + 1e-05)
        return m0, m1, i0, i1

    m0, m1, i0, i1 = norm_coefs(0)
    coef[0] = both(m0, m1)
    coef[1] = both(i0, i1)
    halo_m, halo_i = halo_both(m0, m1), halo_both(i0, i1)

    def vhat_first(t):
        v = split(x_ref[at(t), :].astype(F32))
        return (v - coef[0][None]) * coef[1][None]

    def act_first(t):
        return vhat_first(t).reshape(tile, chans) * gain1 + shift1

    def silu_first(t):
        a = act_first(t)
        pad[pad_at(t), :] = a * sigmoid(a)

    loop(silu_first)
    sides = []
    for side in range(2):
        a = (ha_recv[side, 0:edge_rows].astype(F32) - halo_m) * halo_i * gain1 + shift1
        sides.append((a * sigmoid(a)).astype(BF16))
    shifts(vbuf, *sides)

    def conv_x(t):
        v = taps(vbuf, w1_ref, t, False)
        inner[at(t), :] = v
        return fold(v), fold(v * v)

    stat_put(1, *loop_sums(conv_x))
    stat_start(1)
    hb_send[0] = edge(inner[...], 0)
    hb_send[1] = edge(inner[...], 7)
    for copy in halo_copies(1, hb_send, hb_recv):
        copy.start()

    m0, m1, i0, i1 = norm_coefs(1)
    coef[2] = both(m0, m1)
    coef[3] = both(i0, i1)
    halo_m, halo_i = halo_both(m0, m1), halo_both(i0, i1)

    def second(t):
        vhat = ((split(inner[at(t), :]) - coef[2][None]) * coef[3][None]).reshape(tile, chans)
        inner[at(t), :] = vhat
        a = vhat * gain2 + shift2
        pad[pad_at(t), :] = a * sigmoid(a)
        d = dsil[at(t), :] * slope(a) * gain2
        delta[at(t), :] = d
        return fold(d), fold(d * vhat)

    stat_put(2, *loop_sums(second))
    stat_start(2)
    hc_send[0] = edge(delta[...], 0)
    hc_send[1] = edge(delta[...], 7)
    for copy in halo_copies(2, hc_send, hc_recv):
        copy.start()

    halo_end(1, hb_send, hb_recv)
    sides = []
    for side in range(2):
        vhat = (hb_recv[side] - halo_m) * halo_i
        vh_halo[side] = vhat
        a = vhat * gain2 + shift2
        sides.append((a * sigmoid(a)).astype(BF16))
    shifts(ubuf, *sides)

    def weight_gradient(buf, y, store):
        for i in range(3):
            for j in range(3):
                block = lax.dot_general(
                    buf[j, 16 * i : 16 * i + pixels], y, (((0,), (0,)), ((), ())),
                    preferred_element_type=F32,
                )
                store(3 * i + j, block)

    if win is None:

        def put(ref):
            def store(tap, block):
                ref[tap] = block

            return store

        weight_gradient(ubuf, g_ref[...], put(d2_ref))
    else:
        (full, core_in, chip_out, chip_in, c_ss, c_rs, q_ss, q_rs) = refs[32:]
        own, off, length = win
        chips = n // 2
        chip, core = me // 2, lax.rem(me, 2)
        mine = pl.ds(pl.multiple_of(off * core, 8), length)
        other = pl.ds(pl.multiple_of(off * (1 - core), 8), length)

        def put(slot):
            def store(tap, block):
                row = tap * chans
                while row < (tap + 1) * chans:
                    q, r = divmod(row, 2 * own)
                    stop = min((tap + 1) * chans, (q + 1) * 2 * own)
                    low = row - tap * chans
                    full[slot, q, r : r + stop - row] = block[low : low + stop - row]
                    row = stop

            return store

        def core_copy(slot):
            return pltpu.make_async_remote_copy(
                src_ref=full.at[slot, :, other, :],
                dst_ref=core_in.at[slot],
                send_sem=c_ss.at[slot],
                recv_sem=c_rs.at[slot],
                device_id={"lon": me + 1 - 2 * core},
                device_id_type=MESH,
            )

        def chip_copy(slot, k):
            to = lax.rem(chip + k, chips)
            return pltpu.make_async_remote_copy(
                src_ref=chip_out.at[slot, to],
                dst_ref=chip_in.at[slot, k],
                send_sem=q_ss.at[slot, k],
                recv_sem=q_rs.at[slot, k],
                device_id={"lon": 2 * to + core},
                device_id_type=MESH,
            )

        def chip_start(slot):
            core_copy(slot).wait()

            def go(k, _):
                to = lax.rem(chip + k, chips)
                chip_out[slot, to] = (full[slot, to, mine, :] + core_in[slot, to]).astype(BF16)
                chip_copy(slot, k).start()
                return 0

            lax.fori_loop(1, chips, go, 0)

        def chip_end(slot, ref):
            def end(k, _):
                chip_copy(slot, k).wait()
                return 0

            lax.fori_loop(1, chips, end, 0)

            def add(k, acc):
                return acc + chip_in[slot, k].astype(F32)

            start = full[slot, chip, mine, :] + core_in[slot, chip]
            ref[...] = lax.fori_loop(1, chips, add, start)

        weight_gradient(ubuf, g_ref[...], put(1))
        core_copy(1).start()

    a0, a1, b0, b1 = stat_end(2)
    coef[4] = both(a0, a1)
    coef[5] = both(b0, b1)
    halo_a, halo_b = halo_both(a0, a1), halo_both(b0, b1)

    def make_dinner(t):
        d = split(delta[at(t), :]) - coef[4][None] - split(inner[at(t), :]) * coef[5][None]
        d = (d * coef[3][None]).reshape(tile, chans)
        pad[pad_at(t), :] = d
        dinn[at(t), :] = d.astype(BF16)

    loop(make_dinner)
    if win is not None:
        chip_start(1)
        weight_gradient(vbuf, dinn[...], put(0))
        core_copy(0).start()
    else:
        weight_gradient(vbuf, dinn[...], put(d1_ref))
    halo_end(2, hc_send, hc_recv)
    sides = [
        ((hc_recv[side] - halo_a - vh_halo[side] * halo_b) * halo_i).astype(BF16)
        for side in range(2)
    ]
    shifts(dbuf, *sides)

    def conv_d(t):
        d = taps(dbuf, w1_ref, t, True) * slope(act_first(t)) * gain1
        delta[at(t), :] = d
        return fold(d), fold(d * vhat_first(t).reshape(tile, chans))

    stat_put(3, *loop_sums(conv_d))
    stat_start(3)
    if win is not None:
        chip_start(0)
    a0, a1, b0, b1 = stat_end(3)
    coef[4] = both(a0, a1)
    coef[5] = both(b0, b1)

    def finish(t):
        d = split(delta[at(t), :]) - coef[4][None] - vhat_first(t) * coef[5][None]
        d = (d * coef[1][None]).reshape(tile, chans)
        out_ref[at(t), :] = (g_ref[at(t), :].astype(F32) + d).astype(BF16)

    loop(finish)
    if win is not None:
        chip_end(1, d2_ref)
        chip_end(0, d1_ref)


def per_device(
    n, scene, grad_out, conv_first, conv_second, gain_first, shift_first, gain_second, shift_second
):
    scenes, height, width, chans = scene.shape
    pixels = scenes * height * width
    win = window(9 * chans, n)
    count = height * width * n * (chans // GROUPS)
    edge_rows = pixels // 8

    def flat(v):
        return jnp.transpose(v, (1, 0, 2, 3)).reshape(pixels, chans)

    params = jnp.concatenate(
        [
            jnp.stack([gain_first, shift_first, gain_second, shift_second]),
            jnp.zeros((4, chans), F32),
        ]
    )
    group = jnp.arange(chans) // (chans // GROUPS)
    mix = (group[:, None] == group[None, :]).astype(F32)
    grad_shape = (9, chans, chans) if win is None else (win[2], chans)
    dma = pltpu.SemaphoreType.DMA
    scratch = [
        pltpu.VMEM((4, 8, chans), F32),
        pltpu.VMEM((4, n, 8, chans), F32),
        pltpu.VMEM((2, 2 * edge_rows, chans), BF16),
        pltpu.VMEM((2, 2 * edge_rows, chans), BF16),
        pltpu.VMEM((2, edge_rows, chans), F32),
        pltpu.VMEM((2, edge_rows, chans), F32),
        pltpu.VMEM((2, edge_rows, chans), F32),
        pltpu.VMEM((2, edge_rows, chans), F32),
        pltpu.VMEM((pixels + 16, chans), F32),
        pltpu.VMEM((3, pixels + 32, chans), BF16),
        pltpu.VMEM((3, pixels + 32, chans), BF16),
        pltpu.VMEM((3, pixels + 32, chans), BF16),
        pltpu.VMEM((3, pixels + 32, chans), BF16),
        pltpu.VMEM((pixels, chans), F32),
        pltpu.VMEM((pixels, chans), F32),
        pltpu.VMEM((pixels, chans), F32),
        pltpu.VMEM((pixels, chans), BF16),
        pltpu.VMEM((6, 16, chans), F32),
        pltpu.VMEM((2, edge_rows, chans), F32),
        dma((4, n)),
        dma((4, n)),
        dma((3, 2)),
        dma((3, 2)),
    ]
    if win is not None:
        own, _, length = win
        chips = n // 2
        scratch += [
            pltpu.VMEM((2, chips, 2 * own, chans), F32),
            pltpu.VMEM((2, chips, length, chans), F32),
            pltpu.VMEM((2, chips, length, chans), BF16),
            pltpu.VMEM((2, chips, length, chans), BF16),
            dma((2,)),
            dma((2,)),
            dma((2, chips)),
            dma((2, chips)),
        ]
    vmem = pl.BlockSpec(memory_space=pltpu.VMEM)
    out, first, second = pl.pallas_call(
        functools.partial(kernel, n, height, count, win),
        out_shape=(
            jax.ShapeDtypeStruct((pixels, chans), BF16),
            jax.ShapeDtypeStruct(grad_shape, F32),
            jax.ShapeDtypeStruct(grad_shape, F32),
        ),
        in_specs=[vmem] * 6,
        out_specs=(vmem, vmem, vmem),
        scratch_shapes=scratch,
        compiler_params=pltpu.CompilerParams(
            collective_id=0, has_side_effects=True, vmem_limit_bytes=56 * 1024 * 1024
        ),
    )(
        flat(scene),
        flat(grad_out),
        conv_first.reshape(9, chans, chans),
        conv_second.reshape(9, chans, chans),
        params,
        mix,
    )
    grad_input = jnp.transpose(out.reshape(height, scenes, width, chans), (1, 0, 2, 3))
    if win is None:
        first, second = (
            lax.psum_scatter(v.reshape(-1), "lon", scatter_dimension=0, tiled=True)
            for v in (first, second)
        )
    else:
        own, off, _ = win
        skip = lax.rem(lax.axis_index("lon"), 2) * (own - off)
        first, second = (
            lax.dynamic_slice_in_dim(v, skip, own, axis=0).reshape(-1) for v in (first, second)
        )
    return grad_input, first, second


def solution(mesh):
    placed = (
        P("groups", None, "lon", None),
        P("groups", None, "lon", None),
        P(),
        P(),
        P(),
        P(),
        P(),
        P(),
    )
    return jax.shard_map(
        functools.partial(per_device, mesh.shape["lon"]),
        mesh=mesh,
        in_specs=placed,
        out_specs=(P("groups", None, "lon", None), P(("groups", "lon")), P(("groups", "lon"))),
        check_vma=False,
    )
```

time: 395 us -> 110 us (0.28); the launches traced: 390 us -> 110 us
  blocking collectives: 119 us -> 0 us
  Pallas kernels: 0 us -> 98.7 us
  waiting for transfers between devices: 98.6 us -> 0 us
  local copies, waits for them, and re-layouts: 82.5 us -> 9.28 us
  matrix products: 31.3 us -> 0 us
  other arithmetic: 29.5 us -> 0.93 us
  between operations: 15 us -> 0.73 us
  starting transfers between devices: 14 us -> 0 us
    psum x4 -> x0, blocking collectives: 119 us -> none  [the longest x2 64.9 us: norm_backward(): lax.psum((group_sums(delta), group_sums(delta * vhat)), 'lon')]
    pallas_call x0 -> x1, Pallas kernels: none -> 98.7 us  [per_device(): pl.pallas_call(functools.partial(kernel, n, height, count, win), out_shap...]
    unnamed x2 -> x0, waiting for transfers between devices: 98.6 us -> none
    dot_general x5 -> x0, matrix products: 31.3 us -> none  [the longest x3 17.5 us: convolve(): jnp.dot(patches_of(padded), kernel.reshape(9 * chans, -1), preferred_elem...]
    concatenate x4 -> x1, local copies, waits for them, and re-layouts: 31.9 us -> 0.62 us  [per_device(): jnp.concatenate([jnp.stack([gain_first, shift_first, gain_second, shift_s...]
    concatenate x8 -> x0, other arithmetic: 16.7 us -> none  [with_halo(): block = jnp.concatenate([low, block, high], axis=dim)]
    another operation x1 -> x4, local copies, waits for them, and re-layouts: 15.2 us -> 0.01 us  [per_device(): jnp.stack([gain_first, shift_first, gain_second, shift_second])]
    ppermute x8 -> x0, starting transfers between devices: 14 us -> none  [the longest x4 11.4 us: with_halo(): lax.ppermute(lax.slice_in_dim(block, 0, width, axis=dim), axis, backward)]
  transfers between devices with their start and end apart: 9 -> 0, of which waited for: 1 -> 0; matrix products, arithmetic and copies ran while one was open for 23% -> 0% of each run, Pallas kernels for 0% -> 0%
where the time goes in v1:
time: 110 us
  Pallas kernels  98.7 us (90%)
  local copies, waits for them, and re-layouts  9.28 us (8%)
    pallas_call x1, Pallas kernels, per_device(): pl.pallas_call(functools.partial(kernel, n, height, count, win), out_shap...  98.7 us
    transpose x2, local copies, waits for them, and re-layouts, flat(): return jnp.transpose(v, (1, 0, 2, 3)).reshape(pixels, chans)  3.91 us

profile of v1, /device:TPU:12, one launch (start us, length us, event | category | flops | bytes accessed | tf_op | source)
XLA Modules:
  0.0 109.7 jit_solution(15357174925562906812)
XLA Ops:
  0.6 0.0 copy-start
  0.6 0.0 copy-start.1
  0.7 0.0 copy-start.2
  0.7 0.0 copy-start.3
  0.7 2.0 %copy.11 = bf16[48,2,8,320]{3,2,1,0:T(8,128)(2,1)} copy(bf16[48,2,8,320]{3,2,0,1:T(8,128)(2,1)} %bitcast.14) | data formatting | bytes 983040 | tf_op jit(solution)/shard_map/transpose | solution.py:451
  2.6 1.9 %copy.12 = bf16[48,2,8,320]{3,2,1,0:T(8,128)(2,1)} copy(bf16[48,2,8,320]{3,2,0,1:T(8,128)(2,1)} %bitcast.15) | data formatting | bytes 983040 | tf_op jit(solution)/shard_map/transpose | solution.py:451
  4.6 0.0 copy-done
  4.6 0.0 copy-done.1
  4.6 0.0 copy-done.2
  4.6 0.0 copy-done.3
  4.7 0.6 concatenate.3.refs_4_
  5.3 0.9 compare_convert_fusion.refs_5_
  6.2 98.7 %shard_map.103 = (bf16[768,320]{1,0:T(8,128)(2,1)}, f32[184,320]{1,0:T(8,128)}, f32[184,320]{1,0:T(8,128)}) custom-call(bf16[768,320]{1,0:T(8,128)(2,1)} %bitcast.10, bf16[768,320]{1,0:T(8,128)(2,1)} %bitcast.11, bf16[9,320,320]{2,1,0:T(8,128)(2,1)} %bitcast.12, bf16[9,320,320]{2,1,0:T(8,128)(2,1)} %bitcast.13, f32[8,320]{1,0:T(8,128)} %concatenate.3.refs_4_, ...), custom_call_target="tpu_custom_call" | custom-call | tf_op jit(solution)/shard_map/pallas_call | solution.py:502
  104.9 1.9 %copy.15 = bf16[48,2,8,320]{3,2,0,1:T(8,128)(2,1)} copy(bf16[48,2,8,320]{3,2,1,0:T(8,128)(2,1)} %bitcast.17) | data formatting | bytes 983040 | tf_op jit(solution)/shard_map/reshape | solution.py:523
  106.9 1.1 constant_dynamic-slice_fusion
  108.0 0.8 reshape.58
  108.8 0.8 reshape.59
  (6 shorter events, 0.0 us)
Async XLA Ops:
  0.6 3.9 %copy-start = (f32[320]{0:T(512)S(1)}, f32[320]{0:T(512)}, u32[]{:S(2)}) copy-start(f32[320]{0:T(512)} %param.12) | copy-start | bytes 3844
  0.6 3.9 %copy-start.1 = (f32[320]{0:T(512)S(1)}, f32[320]{0:T(512)}, u32[]{:S(2)}) copy-start(f32[320]{0:T(512)} %param.13) | copy-start | bytes 3844
  0.7 4.0 %copy-start.2 = (f32[320]{0:T(512)S(1)}, f32[320]{0:T(512)}, u32[]{:S(2)}) copy-start(f32[320]{0:T(512)} %param.14) | copy-start | bytes 3844
  0.7 4.0 %copy-start.3 = (f32[320]{0:T(512)S(1)}, f32[320]{0:T(512)}, u32[]{:S(2)}) copy-start(f32[320]{0:T(512)} %param.15) | copy-start | bytes 3844

commit v2 on v1

--- a/solution.py
+++ b/solution.py
@@ -15,7 +15,7 @@
 
 
 def window(rows, n):
-    if n % 2 or rows % n or (2 * rows // n) % 8:
+    if n % 4 or rows % n or (2 * rows // n) % 8:
         return None
     own = rows // n
     off = own // 8 * 8
@@ -32,14 +32,17 @@
 
 
 def kernel(n, height, eps_count, win, *refs):
-    (x_ref, g_ref, w1_ref, w2_ref, par_ref, mix_ref, out_ref, d1_ref, d2_ref) = refs[:9]
+    (x_raw, g_raw, w1_ref, w2_ref) = refs[:4]
+    gain1, shift1, gain2, shift2 = (ref[...] for ref in refs[4:8])
+    (out_ref, d1_ref, d2_ref) = refs[8:11]
     (
         st_send, st_recv, ha_send, ha_recv, hb_send, hb_recv, hc_send, hc_recv,
         pad, vbuf, ubuf, gbuf, dbuf, inner, dsil, delta, dinn, coef, vh_halo,
-        st_ss, st_rs, h_ss, h_rs,
-    ) = refs[9:32]
+        x_ref, g_ref, mix_ref, st_ss, st_rs, h_ss, h_rs,
+    ) = refs[11:37]
     pixels, chans = x_ref.shape
-    tile = 16 * (height // 3)
+    deep = height // 3
+    tile = 16 * deep
     tiles = pixels // tile
     edge_rows = pixels // 8
     me = lax.axis_index("lon")
@@ -202,11 +205,23 @@
 
         return lax.fori_loop(0, tiles, step, (zero, zero))
 
-    gain1, shift1 = par_ref[0:1], par_ref[1:2]
-    gain2, shift2 = par_ref[2:3], par_ref[3:4]
+    def member(dim):
+        index = lax.broadcasted_iota(jnp.int32, (chans, chans), dim).astype(F32)
+        return jnp.floor((index + 0.5) * (GROUPS / chans))
+
+    def rows_of(t):
+        return pl.ds(t * deep, deep)
+
+    def gather_rows(raw, t):
+        pair = [raw[b, rows_of(t)].astype(F32) for b in range(2)]
+        return jnp.concatenate(pair, axis=1)
 
     def sums_x(t):
-        v = x_ref[at(t), :].astype(F32)
+        v = gather_rows(x_raw, t).reshape(tile, chans)
+        x_ref[at(t), :] = v.astype(BF16)
+        g = gather_rows(g_raw, t).reshape(tile, chans)
+        g_ref[at(t), :] = g.astype(BF16)
+        pad[pad_at(t), :] = g
         return fold(v), fold(v * v)
 
     stat_put(0, *loop_sums(sums_x))
@@ -220,10 +235,7 @@
     for copy in halo_copies(0, ha_send, ha_recv):
         copy.start()
 
-    def pad_g(t):
-        pad[pad_at(t), :] = g_ref[at(t), :].astype(F32)
-
-    loop(pad_g)
+    mix_ref[...] = jnp.where(member(0) == member(1), 1.0, 0.0)
     halo_end(0, ha_send, ha_recv)
     shifts(gbuf, ha_recv[0, edge_rows : 2 * edge_rows], ha_recv[1, edge_rows : 2 * edge_rows])
 
@@ -322,10 +334,14 @@
 
         weight_gradient(ubuf, g_ref[...], put(d2_ref))
     else:
-        (full, core_in, chip_out, chip_in, c_ss, c_rs, q_ss, q_rs) = refs[32:]
+        (full, core_in, pair_out, pair_in, chip_out, chip_in, c_ss, c_rs, p_ss, p_rs, q_ss, q_rs) = (
+            refs[37:]
+        )
         own, off, length = win
         chips = n // 2
+        pairs = chips // 2
         chip, core = me // 2, lax.rem(me, 2)
+        row, side_of = chip // 2, lax.rem(chip, 2)
         mine = pl.ds(pl.multiple_of(off * core, 8), length)
         other = pl.ds(pl.multiple_of(off * (1 - core), 8), length)
 
@@ -351,10 +367,20 @@
                 device_id_type=MESH,
             )
 
+        def pair_copy(slot, k):
+            return pltpu.make_async_remote_copy(
+                src_ref=pair_out.at[slot, k],
+                dst_ref=pair_in.at[slot, k],
+                send_sem=p_ss.at[slot, k],
+                recv_sem=p_rs.at[slot, k],
+                device_id={"lon": 2 * (chip + 1 - 2 * side_of) + core},
+                device_id_type=MESH,
+            )
+
         def chip_copy(slot, k):
-            to = lax.rem(chip + k, chips)
+            to = 2 * lax.rem(row + k, pairs) + side_of
             return pltpu.make_async_remote_copy(
-                src_ref=chip_out.at[slot, to],
+                src_ref=chip_out.at[slot, k],
                 dst_ref=chip_in.at[slot, k],
                 send_sem=q_ss.at[slot, k],
                 recv_sem=q_rs.at[slot, k],
@@ -362,29 +388,40 @@
                 device_id_type=MESH,
             )
 
+        def pair_start(slot):
+            core_copy(slot).wait()
+
+            def go(k, _):
+                to = 2 * lax.rem(row + k, pairs) + 1 - side_of
+                pair_out[slot, k - 1] = (
+                    full[slot, to, mine, :] + core_in[slot, to]
+                ).astype(BF16)
+                pair_copy(slot, k - 1).start()
+                return 0
+
+            lax.fori_loop(1, pairs + 1, go, 0)
+
+        def pair_sum(slot, k):
+            to = 2 * lax.rem(row + k, pairs) + side_of
+            pair_copy(slot, k - 1).wait()
+            return full[slot, to, mine, :] + core_in[slot, to] + pair_in[slot, k - 1].astype(F32)
+
         def chip_start(slot):
-            core_copy(slot).wait()
-
             def go(k, _):
-                to = lax.rem(chip + k, chips)
-                chip_out[slot, to] = (full[slot, to, mine, :] + core_in[slot, to]).astype(BF16)
+                chip_out[slot, k] = pair_sum(slot, k).astype(BF16)
                 chip_copy(slot, k).start()
                 return 0
 
-            lax.fori_loop(1, chips, go, 0)
+            lax.fori_loop(1, pairs, go, 0)
 
         def chip_end(slot, ref):
-            def end(k, _):
+            def add(k, acc):
                 chip_copy(slot, k).wait()
-                return 0
-
-            lax.fori_loop(1, chips, end, 0)
-
-            def add(k, acc):
                 return acc + chip_in[slot, k].astype(F32)
 
-            start = full[slot, chip, mine, :] + core_in[slot, chip]
-            ref[...] = lax.fori_loop(1, chips, add, start)
+            total = lax.fori_loop(1, pairs, add, pair_sum(slot, pairs))
+            skip = own - off
+            ref[...] = jnp.where(core == 0, total[0:own], total[skip : skip + own])
 
         weight_gradient(ubuf, g_ref[...], put(1))
         core_copy(1).start()
@@ -402,7 +439,7 @@
 
     loop(make_dinner)
     if win is not None:
-        chip_start(1)
+        pair_start(1)
         weight_gradient(vbuf, dinn[...], put(0))
         core_copy(0).start()
     else:
@@ -413,6 +450,9 @@
         for side in range(2)
     ]
     shifts(dbuf, *sides)
+    if win is not None:
+        chip_start(1)
+        pair_start(0)
 
     def conv_d(t):
         d = taps(dbuf, w1_ref, t, True) * slope(act_first(t)) * gain1
@@ -429,8 +469,9 @@
 
     def finish(t):
         d = split(delta[at(t), :]) - coef[4][None] - vhat_first(t) * coef[5][None]
-        d = (d * coef[1][None]).reshape(tile, chans)
-        out_ref[at(t), :] = (g_ref[at(t), :].astype(F32) + d).astype(BF16)
+        d = d * coef[1][None] + split(g_ref[at(t), :].astype(F32))
+        for b in range(2):
+            out_ref[b, rows_of(t)] = d[:, 8 * b : 8 * b + 8].astype(BF16)
 
     loop(finish)
     if win is not None:
@@ -447,18 +488,7 @@
     count = height * width * n * (chans // GROUPS)
     edge_rows = pixels // 8
 
-    def flat(v):
-        return jnp.transpose(v, (1, 0, 2, 3)).reshape(pixels, chans)
-
-    params = jnp.concatenate(
-        [
-            jnp.stack([gain_first, shift_first, gain_second, shift_second]),
-            jnp.zeros((4, chans), F32),
-        ]
-    )
-    group = jnp.arange(chans) // (chans // GROUPS)
-    mix = (group[:, None] == group[None, :]).astype(F32)
-    grad_shape = (9, chans, chans) if win is None else (win[2], chans)
+    grad_shape = (9, chans, chans) if win is None else (win[0], chans)
     dma = pltpu.SemaphoreType.DMA
     scratch = [
         pltpu.VMEM((4, 8, chans), F32),
@@ -480,6 +510,9 @@
         pltpu.VMEM((pixels, chans), BF16),
         pltpu.VMEM((6, 16, chans), F32),
         pltpu.VMEM((2, edge_rows, chans), F32),
+        pltpu.VMEM((pixels, chans), BF16),
+        pltpu.VMEM((pixels, chans), BF16),
+        pltpu.VMEM((chans, chans), F32),
         dma((4, n)),
         dma((4, n)),
         dma((3, 2)),
@@ -488,51 +521,48 @@
     if win is not None:
         own, _, length = win
         chips = n // 2
+        pairs = chips // 2
         scratch += [
             pltpu.VMEM((2, chips, 2 * own, chans), F32),
             pltpu.VMEM((2, chips, length, chans), F32),
-            pltpu.VMEM((2, chips, length, chans), BF16),
-            pltpu.VMEM((2, chips, length, chans), BF16),
+            pltpu.VMEM((2, pairs, length, chans), BF16),
+            pltpu.VMEM((2, pairs, length, chans), BF16),
+            pltpu.VMEM((2, pairs, length, chans), BF16),
+            pltpu.VMEM((2, pairs, length, chans), BF16),
             dma((2,)),
             dma((2,)),
-            dma((2, chips)),
-            dma((2, chips)),
+            dma((2, pairs)),
+            dma((2, pairs)),
+            dma((2, pairs)),
+            dma((2, pairs)),
         ]
     vmem = pl.BlockSpec(memory_space=pltpu.VMEM)
     out, first, second = pl.pallas_call(
         functools.partial(kernel, n, height, count, win),
         out_shape=(
-            jax.ShapeDtypeStruct((pixels, chans), BF16),
+            jax.ShapeDtypeStruct(scene.shape, BF16),
             jax.ShapeDtypeStruct(grad_shape, F32),
             jax.ShapeDtypeStruct(grad_shape, F32),
         ),
-        in_specs=[vmem] * 6,
+        in_specs=[vmem] * 8,
         out_specs=(vmem, vmem, vmem),
         scratch_shapes=scratch,
         compiler_params=pltpu.CompilerParams(
             collective_id=0, has_side_effects=True, vmem_limit_bytes=56 * 1024 * 1024
         ),
     )(
-        flat(scene),
-        flat(grad_out),
+        scene,
+        grad_out,
         conv_first.reshape(9, chans, chans),
         conv_second.reshape(9, chans, chans),
-        params,
-        mix,
+        *(v.reshape(1, chans) for v in (gain_first, shift_first, gain_second, shift_second)),
     )
-    grad_input = jnp.transpose(out.reshape(height, scenes, width, chans), (1, 0, 2, 3))
     if win is None:
         first, second = (
             lax.psum_scatter(v.reshape(-1), "lon", scatter_dimension=0, tiled=True)
             for v in (first, second)
         )
-    else:
-        own, off, _ = win
-        skip = lax.rem(lax.axis_index("lon"), 2) * (own - off)
-        first, second = (
-            lax.dynamic_slice_in_dim(v, skip, own, axis=0).reshape(-1) for v in (first, second)
-        )
-    return grad_input, first, second
+    return out, first.reshape(-1), second.reshape(-1)
 
 
 def solution(mesh):

time: 110 us -> 92 us (0.84); the launches traced: 110 us -> 90.3 us
  Pallas kernels: 98.7 us -> 79.1 us
  local copies, waits for them, and re-layouts: 9.28 us -> 10.5 us
    pallas_call x1, Pallas kernels: 98.7 us -> 79.1 us  [per_device(): pl.pallas_call(functools.partial(kernel, n, height, count, win), out_shap...]
    reshape x3 -> x6, local copies, waits for them, and re-layouts: 3.63 us -> 8.58 us  [the longest x4 4.98 us: per_device(): v.reshape(1, chans)]
    transpose x2 -> x0, local copies, waits for them, and re-layouts: 3.91 us -> none  [flat(): return jnp.transpose(v, (1, 0, 2, 3)).reshape(pixels, chans)]
    unnamed x8 -> x1, local copies, waits for them, and re-layouts: 0.02 us -> 1.94 us
where the time goes in v2:
time: 92 us; the launch traced here: 90.3 us
  Pallas kernels  79.1 us (86%)
  local copies, waits for them, and re-layouts  10.5 us (11%)
    pallas_call x1, Pallas kernels, per_device(): pl.pallas_call(functools.partial(kernel, n, height, count, win), out_shap...  79.1 us
    reshape x4, local copies, waits for them, and re-layouts, per_device(): v.reshape(1, chans)  4.98 us
    reshape x2, local copies, waits for them, and re-layouts, per_device(): return (out, first.reshape(-1), second.reshape(-1))  3.6 us
    unnamed x1, local copies, waits for them, and re-layouts  1.94 us

profile of v2, /device:TPU:12, one launch (start us, length us, event | category | flops | bytes accessed | tf_op | source)
XLA Modules:
  0.0 90.3 jit_solution(3401150810965425747)
XLA Ops:
  0.6 1.2 %reshape.32.refs_4_ = f32[1,320]{1,0:T(1,128)} reshape(f32[320]{0:T(512)} %param.12) | data formatting | bytes 2560 | tf_op jit(solution)/shard_map/reshape | solution.py:558
  1.9 1.2 %reshape.33.refs_5_ = f32[1,320]{1,0:T(1,128)} reshape(f32[320]{0:T(512)} %param.13) | data formatting | bytes 2560 | tf_op jit(solution)/shard_map/reshape | solution.py:558
  3.1 1.2 %reshape.34.refs_6_ = f32[1,320]{1,0:T(1,128)} reshape(f32[320]{0:T(512)} %param.14) | data formatting | bytes 2560 | tf_op jit(solution)/shard_map/reshape | solution.py:558
  4.4 1.2 %reshape.35.refs_7_ = f32[1,320]{1,0:T(1,128)} reshape(f32[320]{0:T(512)} %param.15) | data formatting | bytes 2560 | tf_op jit(solution)/shard_map/reshape | solution.py:558
  5.6 79.1 %shard_map.103 = (bf16[2,48,8,320]{3,2,1,0:T(8,128)(2,1)}, f32[180,320]{1,0:T(8,128)}, f32[180,320]{1,0:T(8,128)}) custom-call(bf16[2,48,8,320]{3,2,1,0:T(8,128)(2,1)} %refs_0_.1, bf16[2,48,8,320]{3,2,1,0:T(8,128)(2,1)} %refs_1_.1, bf16[9,320,320]{2,1,0:T(8,128)(2,1)} %bitcast.2, bf16[9,320,320]{2,1,0:T(8,128)(2,1)} %bitcast.3, f32[1,320]{1,0:T(1,128)} %reshape.32.refs_4_, ...), custom_call_target="tpu_custom_call" | custom-call | tf_op jit(solution)/shard_map/pallas_call | solution.py:540
  84.8 1.8 %reshape.36 = f32[57600]{0:T(1024)} reshape(f32[180,320]{1,0:T(8,128)} %get-tuple-element.7) | data formatting | bytes 460800 | tf_op jit(solution)/shard_map/reshape | solution.py:565
  86.6 1.8 %reshape.37 = f32[57600]{0:T(1024)} reshape(f32[180,320]{1,0:T(8,128)} %get-tuple-element.8) | data formatting | bytes 460800 | tf_op jit(solution)/shard_map/reshape | solution.py:565
  88.4 1.9 %copy.12 = bf16[2,48,8,320]{3,2,1,0:T(8,128)(2,1)} copy(bf16[2,48,8,320]{3,2,1,0:T(8,128)(2,1)} %get-tuple-element.12) | data formatting | bytes 983040

commit v3 on v2

--- a/solution.py
+++ b/solution.py
@@ -11,7 +11,6 @@
 F32 = jnp.float32
 BF16 = jnp.bfloat16
 MESH = pl.DeviceIdType.MESH
-HIGH = lax.Precision.HIGHEST
 
 
 def window(rows, n):
@@ -32,14 +31,14 @@
 
 
 def kernel(n, height, eps_count, win, *refs):
-    (x_raw, g_raw, w1_ref, w2_ref) = refs[:4]
-    gain1, shift1, gain2, shift2 = (ref[...] for ref in refs[4:8])
+    (x_raw, g_raw, w1_hbm, w2_hbm) = refs[:4]
+    gain1, shift1, gain2, shift2 = (ref[...].reshape(1, -1) for ref in refs[4:8])
     (out_ref, d1_ref, d2_ref) = refs[8:11]
     (
         st_send, st_recv, ha_send, ha_recv, hb_send, hb_recv, hc_send, hc_recv,
         pad, vbuf, ubuf, gbuf, dbuf, inner, dsil, delta, dinn, coef, vh_halo,
-        x_ref, g_ref, mix_ref, st_ss, st_rs, h_ss, h_rs,
-    ) = refs[11:37]
+        x_ref, g_ref, mix_ref, w1_ref, w2_ref, w_sems, st_ss, st_rs, h_ss, h_rs,
+    ) = refs[11:40]
     pixels, chans = x_ref.shape
     deep = height // 3
     tile = 16 * deep
@@ -57,7 +56,11 @@
         )
         return 0
 
+    fetch_first = pltpu.make_async_copy(w1_hbm, w1_ref, w_sems.at[0])
+    fetch_second = pltpu.make_async_copy(w2_hbm, w2_ref, w_sems.at[1])
     barrier = pltpu.get_barrier_semaphore()
+    fetch_second.start()
+    fetch_first.start()
     lax.fori_loop(1, n, greet, 0)
 
     def stat_copy(rnd, k):
@@ -98,10 +101,14 @@
             return acc + st_recv[rnd, k]
 
         total = lax.fori_loop(1, n, add, st_recv[rnd, 0])
-        means = (
-            jnp.dot(total, mix_ref[...], precision=HIGH, preferred_element_type=F32)
-            * (1.0 / eps_count)
-        )
+        high = total.astype(BF16)
+        rest = total - high.astype(F32)
+        middle = rest.astype(BF16)
+        low = (rest - middle.astype(F32)).astype(BF16)
+        means = sum(
+            jnp.dot(piece, mix_ref[...], preferred_element_type=F32)
+            for piece in (low, middle, high)
+        ) * (1.0 / eps_count)
         return [means[r : r + 1] for r in range(4)]
 
     def halo_copies(rnd, send, recv):
@@ -124,15 +131,9 @@
         for copy in copies:
             copy.wait_recv()
 
-    def pick(column, dtype):
-        r = lax.broadcasted_iota(jnp.int32, (edge_rows, pixels), 0)
-        p = lax.broadcasted_iota(jnp.int32, (edge_rows, pixels), 1)
-        return jnp.where(p == 8 * r + column, 1.0, 0.0).astype(dtype)
-
-    def edge(value, column):
-        if value.dtype == BF16:
-            return jnp.dot(pick(column, BF16), value, preferred_element_type=F32).astype(BF16)
-        return jnp.dot(pick(column, F32), value, precision=HIGH, preferred_element_type=F32)
+    def edge(ref, column, start=0):
+        tiles_of_eight = ref[start : start + pixels].reshape(edge_rows, 8, chans)
+        return tiles_of_eight[:, column, :]
 
     def both(first, second):
         return jnp.concatenate(
@@ -196,8 +197,14 @@
 
         lax.fori_loop(0, tiles, step, 0)
 
-    def loop_sums(body):
+    def loop_sums(body, between=None):
         zero = jnp.zeros((16, chans), F32)
+        if between is not None:
+            partial = lax.fori_loop(
+                0, tiles - 1, lambda t, c: tuple(x + y for x, y in zip(c, body(t))), (zero, zero)
+            )
+            between()
+            return tuple(x + y for x, y in zip(partial, body(tiles - 1)))
 
         def step(t, carry):
             a, b = body(t)
@@ -219,6 +226,7 @@
     def sums_x(t):
         v = gather_rows(x_raw, t).reshape(tile, chans)
         x_ref[at(t), :] = v.astype(BF16)
+        delta[at(t), :] = v
         g = gather_rows(g_raw, t).reshape(tile, chans)
         g_ref[at(t), :] = g.astype(BF16)
         pad[pad_at(t), :] = g
@@ -226,8 +234,8 @@
 
     stat_put(0, *loop_sums(sums_x))
     for side, column in ((0, 0), (1, 7)):
-        ha_send[side, 0:edge_rows] = edge(x_ref[...], column)
-        ha_send[side, edge_rows : 2 * edge_rows] = edge(g_ref[...], column)
+        ha_send[side, 0:edge_rows] = edge(delta, column).astype(BF16)
+        ha_send[side, edge_rows : 2 * edge_rows] = edge(pad, column, 8).astype(BF16)
     pad[0:8] = jnp.zeros((8, chans), F32)
     pad[pixels + 8 : pixels + 16] = jnp.zeros((8, chans), F32)
     pl.semaphore_wait(barrier, n - 1)
@@ -235,13 +243,14 @@
     for copy in halo_copies(0, ha_send, ha_recv):
         copy.start()
 
-    mix_ref[...] = jnp.where(member(0) == member(1), 1.0, 0.0)
+    mix_ref[...] = jnp.where(member(0) == member(1), 1.0, 0.0).astype(BF16)
     halo_end(0, ha_send, ha_recv)
     shifts(gbuf, ha_recv[0, edge_rows : 2 * edge_rows], ha_recv[1, edge_rows : 2 * edge_rows])
 
     def conv_g(t):
         dsil[at(t), :] = taps(gbuf, w2_ref, t, True)
 
+    fetch_second.wait()
     loop(conv_g)
 
     def norm_coefs(rnd):
@@ -278,10 +287,11 @@
         inner[at(t), :] = v
         return fold(v), fold(v * v)
 
+    fetch_first.wait()
     stat_put(1, *loop_sums(conv_x))
     stat_start(1)
-    hb_send[0] = edge(inner[...], 0)
-    hb_send[1] = edge(inner[...], 7)
+    hb_send[0] = edge(inner, 0)
+    hb_send[1] = edge(inner, 7)
     for copy in halo_copies(1, hb_send, hb_recv):
         copy.start()
 
@@ -301,8 +311,8 @@
 
     stat_put(2, *loop_sums(second))
     stat_start(2)
-    hc_send[0] = edge(delta[...], 0)
-    hc_send[1] = edge(delta[...], 7)
+    hc_send[0] = edge(delta, 0)
+    hc_send[1] = edge(delta, 7)
     for copy in halo_copies(2, hc_send, hc_recv):
         copy.start()
 
@@ -335,7 +345,7 @@
         weight_gradient(ubuf, g_ref[...], put(d2_ref))
     else:
         (full, core_in, pair_out, pair_in, chip_out, chip_in, c_ss, c_rs, p_ss, p_rs, q_ss, q_rs) = (
-            refs[37:]
+            refs[40:]
         )
         own, off, length = win
         chips = n // 2
@@ -450,16 +460,18 @@
         for side in range(2)
     ]
     shifts(dbuf, *sides)
-    if win is not None:
-        chip_start(1)
-        pair_start(0)
 
     def conv_d(t):
         d = taps(dbuf, w1_ref, t, True) * slope(act_first(t)) * gain1
         delta[at(t), :] = d
         return fold(d), fold(d * vhat_first(t).reshape(tile, chans))
 
-    stat_put(3, *loop_sums(conv_d))
+    def between():
+        if win is not None:
+            chip_start(1)
+            pair_start(0)
+
+    stat_put(3, *loop_sums(conv_d, between))
     stat_start(3)
     if win is not None:
         chip_start(0)
@@ -512,7 +524,10 @@
         pltpu.VMEM((2, edge_rows, chans), F32),
         pltpu.VMEM((pixels, chans), BF16),
         pltpu.VMEM((pixels, chans), BF16),
-        pltpu.VMEM((chans, chans), F32),
+        pltpu.VMEM((chans, chans), BF16),
+        pltpu.VMEM((9, chans, chans), BF16),
+        pltpu.VMEM((9, chans, chans), BF16),
+        dma((2,)),
         dma((4, n)),
         dma((4, n)),
         dma((3, 2)),
@@ -544,7 +559,7 @@
             jax.ShapeDtypeStruct(grad_shape, F32),
             jax.ShapeDtypeStruct(grad_shape, F32),
         ),
-        in_specs=[vmem] * 8,
+        in_specs=[vmem] * 2 + [pl.BlockSpec(memory_space=pl.ANY)] * 2 + [vmem] * 4,
         out_specs=(vmem, vmem, vmem),
         scratch_shapes=scratch,
         compiler_params=pltpu.CompilerParams(
@@ -555,7 +570,10 @@
         grad_out,
         conv_first.reshape(9, chans, chans),
         conv_second.reshape(9, chans, chans),
-        *(v.reshape(1, chans) for v in (gain_first, shift_first, gain_second, shift_second)),
+        gain_first,
+        shift_first,
+        gain_second,
+        shift_second,
     )
     if win is None:
         first, second = (

time: 92 us -> 85 us (0.924)
  local copies, waits for them, and re-layouts: 10.5 us -> 5.54 us
  Pallas kernels: 79.1 us -> 77.9 us
    reshape x4 -> x0, local copies, waits for them, and re-layouts: 4.98 us -> none  [per_device(): v.reshape(1, chans)]
    pallas_call x1, Pallas kernels: 79.1 us -> 77.9 us  [per_device(): pl.pallas_call(functools.partial(kernel, n, height, count, win), out_shap...]
where the time goes in v3:
time: 85 us; the launch traced here: 84 us
  Pallas kernels  77.9 us (92%)
  local copies, waits for them, and re-layouts  5.54 us (7%)
    pallas_call x1, Pallas kernels, per_device(): pl.pallas_call(functools.partial(kernel, n, height, count, win), out_shap...  77.9 us
    reshape x2, local copies, waits for them, and re-layouts, per_device(): return (out, first.reshape(-1), second.reshape(-1))  3.6 us
    unnamed x1, local copies, waits for them, and re-layouts  1.94 us

profile of v3, /device:TPU:12, one launch (start us, length us, event | category | flops | bytes accessed | tf_op | source)
XLA Modules:
  0.0 84.0 jit_solution(150335643384423000)
XLA Ops:
  0.6 77.9 %shard_map.103 = (bf16[2,48,8,320]{3,2,1,0:T(8,128)(2,1)}, f32[180,320]{1,0:T(8,128)}, f32[180,320]{1,0:T(8,128)}) custom-call(bf16[2,48,8,320]{3,2,1,0:T(8,128)(2,1)} %refs_0_.1, bf16[2,48,8,320]{3,2,1,0:T(8,128)(2,1)} %refs_1_.1, bf16[9,320,320]{2,1,0:T(8,128)(2,1)} %bitcast.2, bf16[9,320,320]{2,1,0:T(8,128)(2,1)} %bitcast.3, f32[320]{0:T(512)} %refs_4_.1, ...), custom_call_target="tpu_custom_call" | custom-call | tf_op jit(solution)/shard_map/pallas_call | solution.py:555
  78.5 1.8 %reshape.20 = f32[57600]{0:T(1024)} reshape(f32[180,320]{1,0:T(8,128)} %get-tuple-element.7) | data formatting | bytes 460800 | tf_op jit(solution)/shard_map/reshape | solution.py:583
  80.3 1.8 %reshape.21 = f32[57600]{0:T(1024)} reshape(f32[180,320]{1,0:T(8,128)} %get-tuple-element.8) | data formatting | bytes 460800 | tf_op jit(solution)/shard_map/reshape | solution.py:583
  82.1 1.9 %copy.12 = bf16[2,48,8,320]{3,2,1,0:T(8,128)(2,1)} copy(bf16[2,48,8,320]{3,2,1,0:T(8,128)(2,1)} %get-tuple-element.12) | data formatting | bytes 983040
